TPU v7x, 32 devices: a whole 2x2x4 slice. The times are simulated.
32 devices in a mesh: sec: 4 (over x, core), row: 4 (over z), col: 2 (over y).
Axes of the slice: x: 2, y: 2, z: 4, core: 2. Of those that a mesh axis runs over, the one named last changes fastest.
Arguments:
- images: float32 [4, 1024, 512], P('sec', 'row', 'col'), may hold values from -6 to 6
- stiffness: float32 [4, 1024, 512], P('sec', 'row', 'col'), may hold values from 0.1 to 1
Outputs:
- tensor: float32 [5, 4, 1024, 512], P(None, 'sec', 'row', 'col')
- field: float32 [2, 4, 1024, 512], P(None, 'sec', 'row', 'col')
All inputs are finite; a program needn't handle non-finite values.
Results may differ from a plain program's by a relative error of at most 0.00002.
Values sent between devices are 32-bit elements; how exact they have to be, the bound alone decides.
A program may use at most 64 MiB of HBM per device.

v0:
```python
import functools

import jax
import jax.numpy as jnp
from jax import lax
from jax.experimental import pallas as pl
from jax.experimental.pallas import tpu as pltpu
from jax.sharding import PartitionSpec as P

RADIUS = 4
SWEEPS = 4
ROUNDS = 2
COUPLING = 0.25
MESH = pl.DeviceIdType.MESH

LANES = 128
HALO = 16
EDGE = HALO + 8
SLOT = 16
CHUNK = 64
FOLD = LANES // (2 * SLOT)

(
    TILE_B, ROW_A_UP, ROW_A_DOWN, ROW_S_UP, ROW_S_DOWN, FWD_TOP, FWD_BOTTOM, COL_RIGHT, COL_LEFT,
    FWD_RIGHT, FWD_LEFT,
) = range(11)
KINDS = 11


def lane_roll(x, shift):
    return pltpu.roll(x, shift % x.shape[1], 1)


def shifted(blocks, shift, lane):
    rolled = [lane_roll(x, shift) for x in blocks]
    out = []
    for k, here in enumerate(rolled):
        if shift > 0:
            out.append(jnp.where(lane < shift, rolled[k - 1], here))
        else:
            out.append(jnp.where(lane >= LANES + shift, rolled[(k + 1) % len(rolled)], here))
    return out


def add(*terms):
    return [sum(xs[1:], xs[0]) for xs in zip(*terms)]


def kernel(
    counts, images, stiff, tensor_out, field_out,
    a, b, s, q, gx, gy, pr, p3, tt, ua, ub, uc, va, vb, vc, ex, ey, g0, g1, field, last_field,
    send_right, send_left, got_left, got_right, next_left, next_right,
    rim, rim_before, rim_after, main_before, main_after,
    local_sem, send_sem, recv_sem, chunk_send, chunk_recv,
):
    sec, row, col = (lax.axis_index(name) for name in ("sec", "row", "col"))
    n_sec, n_row, n_col = counts
    rows, width = images.shape[1], images.shape[2]
    nb, total, _ = a.shape
    nw = nb - 1
    has_prev, has_next = sec > 0, sec < n_sec - 1
    has_up, has_down = row > 0, row < n_row - 1
    has_left, has_right = col > 0, col < n_col - 1
    sides = (
        (has_prev, (sec - 1, row, col)), (has_next, (sec + 1, row, col)),
        (has_up, (sec, row - 1, col)), (has_down, (sec, row + 1, col)),
        (has_left, (sec, row, col - 1)), (has_right, (sec, row, col + 1)),
    )
    prev_id, next_id, up_id, down_id, left_id, right_id = (side[1] for side in sides)
    end = EDGE + rows
    first, last = 8, total - 8
    inner = pl.ds(EDGE, rows)
    main = pl.ds(0, nw)
    top, bottom = pl.ds(EDGE - HALO, HALO), pl.ds(end, HALO)
    piece = (last - first) // FOLD

    def remote(src, dst, k, device, part=0):
        return pltpu.make_async_remote_copy(
            src_ref=src, dst_ref=dst, send_sem=send_sem.at[k, part],
            recv_sem=recv_sem.at[k, part], device_id=device, device_id_type=MESH,
        )

    def columns(k):
        return pl.ds(k * LANES, LANES)

    loads = [
        pltpu.make_async_copy(src.at[0, :, columns(k)], dst.at[k, inner], local_sem.at[i, k])
        for i, (src, dst) in enumerate(((images, a), (stiff, s)))
        for k in range(nw)
    ]
    for copy in loads:
        copy.start()
    barrier = pltpu.get_barrier_semaphore()
    for there, device in sides:
        @pl.when(there)
        def _():
            pl.semaphore_signal(barrier, inc=1, device_id=device, device_id_type=MESH)

    def clear(ref):
        ref[...] = jnp.zeros(ref.shape, jnp.float32)

    @pl.when(jnp.logical_not(has_up))
    def _():
        clear(a.at[main, top])
        clear(s.at[main, top])

    @pl.when(jnp.logical_not(has_down))
    def _():
        clear(a.at[main, bottom])
        clear(s.at[main, bottom])

    @pl.when(jnp.logical_not(has_left))
    def _():
        clear(got_left)

    @pl.when(jnp.logical_not(has_right))
    def _():
        clear(got_right)

    @pl.when(jnp.logical_not(has_next))
    def _():
        clear(b)
        clear(next_left)
        clear(next_right)
        clear(rim_after)
        clear(main_after)

    @pl.when(jnp.logical_not(has_prev))
    def _():
        clear(rim_before)
        clear(main_before)

    for start in (0, total - 8):
        for ref in (a, q):
            clear(ref.at[:, pl.ds(start, 8)])
        for ref in (pr, p3):
            clear(ref.at[:, :, pl.ds(start, 8)])
    for start in (8, total - 16):
        for ref in (g0, g1, field):
            clear(ref.at[:, :, pl.ds(start, 8)])

    pl.semaphore_wait(barrier, sum(jnp.where(there, 1, 0) for there, _device in sides))

    def by_block(src, at, dst, to, k, device):
        return [
            remote(src.at[0, at, columns(p)], dst.at[p, to], k, device, p) for p in range(nw)
        ]

    low, high = pl.ds(0, HALO), pl.ds(rows - HALO, HALO)
    tile_b = by_block(images, pl.ds(0, rows), b, inner, TILE_B, prev_id)
    up = by_block(stiff, low, s, bottom, ROW_S_UP, up_id)
    up += by_block(images, low, a, bottom, ROW_A_UP, up_id)
    down = by_block(stiff, high, s, top, ROW_S_DOWN, down_id)
    down += by_block(images, high, a, top, ROW_A_DOWN, down_id)
    col_right = remote(send_right, got_left, COL_RIGHT, right_id)
    col_left = remote(send_left, got_right, COL_LEFT, left_id)
    forward_rows = [
        remote(a.at[main, top], b.at[main, top], FWD_TOP, prev_id),
        remote(a.at[main, bottom], b.at[main, bottom], FWD_BOTTOM, prev_id),
    ]
    forward_cols = [
        remote(got_left, next_left, FWD_LEFT, prev_id),
        remote(got_right, next_right, FWD_RIGHT, prev_id),
    ]

    def when_start(there, copies):
        @pl.when(there)
        def _():
            for copy in copies:
                copy.start()

    def when_got(there, copies):
        @pl.when(there)
        def _():
            for copy in copies:
                copy.wait_recv()

    def when_sent(there, copies):
        @pl.when(there)
        def _():
            for copy in copies:
                copy.wait_send()

    when_start(has_up, up)
    when_start(has_down, down)
    when_start(has_prev, tile_b)
    for copy in loads:
        copy.wait()
    when_got(has_up, down)
    when_got(has_down, up)
    when_start(has_prev, forward_rows)

    def lanes_of(count):
        return lax.broadcasted_iota(jnp.int32, (count, LANES), 1)

    lane = lanes_of(piece)

    def packed(block, at):
        out = jnp.zeros((piece, LANES), jnp.float32)
        for j in range(FOLD):
            span = pl.ds(first + j * piece, piece)
            for k, ref in enumerate((a, s)):
                low = (2 * j + k) * SLOT
                moved = lane_roll(ref[block, span, :], low - at)
                out = jnp.where((lane >= low) & (lane < low + SLOT), moved, out)
        return out

    def unpack(ref, left, right, k):
        for j in range(FOLD):
            low = (2 * j + k) * SLOT
            from_right = jnp.where(lane < SLOT, lane_roll(right[...], -low), 0.0)
            from_left = lane_roll(left[...], LANES - SLOT - low)
            ref[nw, pl.ds(first + j * piece, piece), :] = jnp.where(
                lane >= LANES - SLOT, from_left, from_right
            )

    @pl.when(has_right)
    def _():
        send_right[...] = packed(nw - 1, LANES - SLOT)
        col_right.start()

    @pl.when(has_left)
    def _():
        send_left[...] = packed(0, 0)
        col_left.start()

    when_got(has_left, [col_right])
    when_got(has_right, [col_left])
    when_start(has_prev, forward_cols)
    unpack(a, got_left, got_right, 0)
    unpack(s, got_left, got_right, 1)

    def blocks(low, high, step, body):
        def one(i, carry):
            body(pl.multiple_of(low + i * step, 8), step)
            return carry

        count = (high - low) // step
        lax.fori_loop(0, count, one, 0)
        rest = high - low - count * step
        if rest:
            body(low + count * step, rest)

    def get(ref, r, step, *lead):
        return [ref[(*lead, k, pl.ds(r, step), slice(None))] for k in range(nb)]

    def put(ref, values, r, step, *lead):
        for k, value in enumerate(values):
            ref[(*lead, k, pl.ds(r, step), slice(None))] = value

    def gradient_block(r, step):
        lane = lanes_of(step)
        rr = lax.broadcasted_iota(jnp.int32, (step, LANES), 0) + r
        row_ok = ((rr >= EDGE) | has_up) & ((rr < end) | has_down)
        rim_ok = ((lane < LANES // 2) & has_right) | ((lane >= LANES // 2) & has_left)
        masks = [row_ok] * nw + [row_ok & rim_ok]
        mid = get(a, r, step)
        after, before = shifted(mid, -1, lane), shifted(mid, 1, lane)
        under, over = get(a, r + 1, step), get(a, r - 1, step)
        dx = [jnp.where(m, (x - y) * 0.5, 0.0) for m, x, y in zip(masks, after, before)]
        dy = [jnp.where(m, (x - y) * 0.5, 0.0) for m, x, y in zip(masks, under, over)]
        put(gx, dx, r, step)
        put(gy, dy, r, step)
        put(pr, [x * x for x in dx], r, step, 0)
        put(pr, [x * y for x, y in zip(dx, dy)], r, step, 1)
        put(pr, [y * y for y in dy], r, step, 2)
        put(q, [jnp.sqrt(x) for x in get(s, r, step)], r, step)

    blocks(first, last, 16, gradient_block)

    def three_rows(k):
        def body(r, step):
            put(p3, add(*(get(pr, r + d, step, k) for d in (-1, 0, 1))), r, step, k)

        return body

    scale = jnp.where(has_next, jnp.float32(1.0), jnp.float32(0.0))
    scale = scale * (1.0 / float((2 * RADIUS + 1) ** 2))

    def window_mean(k, r, step):
        lane = lanes_of(step)
        summed = add(*(get(p3, r + d, step, k) for d in (-3, 0, 3)))
        summed = add(summed, shifted(summed, 1, lane), shifted(summed, -1, lane))
        summed = add(summed, shifted(summed, 3, lane), shifted(summed, -3, lane))
        value = [x * scale for x in summed]
        put(tt, value, r, step, k)
        return value

    def three_first(r, step):
        for k in range(3):
            three_rows(k)(r, step)

    blocks(first, last, 16, three_first)

    def mean_first(r, step):
        for k in range(3):
            window_mean(k, r, step)

    blocks(16, total - 16, 16, mean_first)

    when_got(has_next, tile_b + forward_rows + forward_cols)
    unpack(b, next_left, next_right, 0)

    def change_block(r, step):
        change = [x - y for x, y in zip(get(b, r, step), get(a, r, step))]
        put(pr, [x * y for x, y in zip(get(gx, r, step), change)], r, step, 3)
        put(pr, [x * y for x, y in zip(get(gy, r, step), change)], r, step, 4)

    blocks(first, last, 32, change_block)

    def three_second(r, step):
        for k in (3, 4):
            three_rows(k)(r, step)

    blocks(first, last, 16, three_second)

    def tensor_block(r, step):
        lane = lanes_of(step)
        parts = [get(tt, r, step, k) for k in range(3)]
        parts += [window_mean(k, r, step) for k in (3, 4)]
        mid = get(q, r, step)
        around = add(
            get(q, r - 1, step), get(q, r + 1, step), shifted(mid, 1, lane), shifted(mid, -1, lane)
        )
        for k in range(nb):
            xx, xy, yy, xt, yt = (part[k] for part in parts)
            diag = mid[k] * around[k] + 2.0 * COUPLING
            one, two = xx + diag, yy + diag
            inverse = 1.0 / (one * two - xy * xy)
            ca, cb, cc = two * inverse, xy * inverse, one * inverse
            x, y = cb * yt - ca * xt, cb * xt - cc * yt
            at = pl.ds(r, step)
            for ref, value in ((va, ca), (vb, cb), (vc, cc)):
                ref[k, at, :] = value * COUPLING
            for ref, value in ((ua, ca), (ub, cb), (uc, cc)):
                ref[k, at, :] = value * mid[k]
            ex[k, at, :] = x
            ey[k, at, :] = y
            g0[0, k, at, :] = x * mid[k]
            g0[1, k, at, :] = y * mid[k]

    def relaxed(source, r, step, x, y):
        lane = lanes_of(step)

        def near(part):
            mid = get(source, r, step, part)
            return add(
                get(source, r - 1, step, part), get(source, r + 1, step, part),
                shifted(mid, 1, lane), shifted(mid, -1, lane),
            )

        nx, ny = near(0), near(1)
        ca, cb, cc = (get(ref, r, step) for ref in (ua, ub, uc))
        return (
            [x[k] + ca[k] * nx[k] - cb[k] * ny[k] for k in range(nb)],
            [y[k] + cc[k] * ny[k] - cb[k] * nx[k] for k in range(nb)],
        )

    def sweep(source, target, scaled=None):
        def body(r, step):
            new = relaxed(source, r, step, get(ex, r, step), get(ey, r, step))
            mid = get(q, r, step) if scaled is not None else None
            for part in range(2):
                if target is not None:
                    put(target, new[part], r, step, part)
                if scaled is not None:
                    put(scaled, [m * x for m, x in zip(mid, new[part])], r, step, part)

        return body

    bounds = list(range(first, last - CHUNK + 1, CHUNK)) + [last]
    chunks = len(bounds) - 1

    def stages(c, bodies, lead, ends):
        for k, body in enumerate(bodies):
            ahead = 8 * (lead - k)
            margin = ends[k == len(bodies) - 1]
            low = first + margin if c == 0 else bounds[c] + ahead
            high = last - margin if c == chunks - 1 else bounds[c + 1] + ahead
            blocks(low, high, 32, body)

    first_round = [tensor_block]
    now, other = g0, g1
    for k in range(1, SWEEPS):
        first_round.append(sweep(now, field if k == SWEEPS - 1 else None, other))
        now, other = other, now

    to_next, to_prev = [], []
    for c in range(chunks):
        stages(c, first_round, SWEEPS - 1, (8, 8))
        low, high = bounds[c], bounds[c + 1]
        folded = pl.ds((low - first) // FOLD, (high - low) // FOLD)
        pack_rim(field, rim, low, high, first, nw)
        rows_sent = pl.ds(max(low, 16), min(high, total - 16) - max(low, 16))

        def moves(rims, mains, device, way):
            pairs = (
                (rim.at[folded], rims.at[folded]),
                (field.at[:, main, rows_sent], mains.at[:, main, rows_sent]),
            )
            return [
                pltpu.make_async_remote_copy(
                    src_ref=src, dst_ref=dst, send_sem=chunk_send.at[way + i, c],
                    recv_sem=chunk_recv.at[way + i, c], device_id=device, device_id_type=MESH,
                )
                for i, (src, dst) in enumerate(pairs)
            ]

        to_next.append(moves(rim_before, main_before, next_id, 0))
        to_prev.append(moves(rim_after, main_after, prev_id, 2))
        when_start(has_next, to_next[c])
        when_start(has_prev, to_prev[c])

    put_tensor = [
        pltpu.make_async_copy(
            tt.at[:, k, inner], tensor_out.at[:, 0, :, columns(k)], local_sem.at[0, k]
        )
        for k in range(nw)
    ]
    for copy in put_tensor:
        copy.start()


    def first_block(r, step):
        at = pl.ds(r, step)

        def beside(part, ref):
            return [
                main_before[part, k, at, :] + main_after[part, k, at, :] for k in range(nw)
            ] + [ref[nw, at, :]]

        x, y = beside(0, gx), beside(1, gy)
        ca, cb, cc = (get(ref, r, step) for ref in (va, vb, vc))
        old_x, old_y = get(ex, r, step), get(ey, r, step)
        new_x = [old_x[k] + ca[k] * x[k] - cb[k] * y[k] for k in range(nb)]
        new_y = [old_y[k] + cc[k] * y[k] - cb[k] * x[k] for k in range(nb)]
        put(ex, new_x, r, step)
        put(ey, new_y, r, step)
        mid = get(q, r, step)
        for part, values in enumerate(relaxed(now, r, step, new_x, new_y)):
            put(other, [m * v for m, v in zip(mid, values)], r, step, part)

    second_round = [first_block]
    source, target = other, now
    for k in range(1, SWEEPS):
        if k == SWEEPS - 1:
            second_round.append(sweep(source, last_field))
        else:
            second_round.append(sweep(source, None, target))
        source, target = target, source

    for c in range(chunks):
        when_got(has_prev, to_next[c])
        when_got(has_next, to_prev[c])
        low, high = bounds[c], bounds[c + 1]
        size = (high - low) // FOLD
        folded = pl.ds((low - first) // FOLD, size)
        both = rim_before[folded, :] + rim_after[folded, :]
        lane = lanes_of(size)
        for j in range(FOLD):
            for k, ref in enumerate((gx, gy)):
                slot = (2 * j + k) * SLOT
                head = jnp.where(lane < 8, lane_roll(both, -slot), 0.0)
                tail = lane_roll(both, LANES - 16 - slot)
                ref[nw, pl.ds(low + j * size, size), :] = jnp.where(
                    lane >= LANES - 8, tail, head
                )
        stages(c, second_round, 0, (8, 16))

    for c in range(chunks):
        when_sent(has_next, to_next[c])
        when_sent(has_prev, to_prev[c])

    put_field = [
        pltpu.make_async_copy(
            last_field.at[:, k, inner], field_out.at[:, 0, :, columns(k)], local_sem.at[1, k]
        )
        for k in range(nw)
    ]
    for copy in put_field:
        copy.start()
    when_sent(has_up, up)
    when_sent(has_down, down)
    when_sent(has_right, [col_right])
    when_sent(has_left, [col_left])
    when_sent(has_prev, tile_b + forward_rows + forward_cols)
    for copy in put_tensor + put_field:
        copy.wait()


def pack_rim(field, rim, low, high, first, nw):
    size = (high - low) // FOLD
    lane = lax.broadcasted_iota(jnp.int32, (size, LANES), 1)
    out = jnp.zeros((size, LANES), jnp.float32)
    for j in range(FOLD):
        at = pl.ds(low + j * size, size)
        for k in range(2):
            slot = (2 * j + k) * SLOT
            block = field[k, nw, at, :]
            head, tail = lane_roll(block, slot), lane_roll(block, slot + SLOT)
            out = jnp.where((lane >= slot) & (lane < slot + 8), head, out)
            out = jnp.where((lane >= slot + 8) & (lane < slot + 16), tail, out)
    rim[pl.ds((low - first) // FOLD, size), :] = out


def local(counts, images, stiffness):
    _, rows, width = images.shape
    nw = width // LANES
    nb = nw + 1
    total = rows + 2 * EDGE
    f32 = jnp.float32
    plane = pltpu.VMEM((nb, total, LANES), f32)
    five = pltpu.VMEM((5, nb, total, LANES), f32)
    pair = pltpu.VMEM((2, nb, total, LANES), f32)
    packet = pltpu.VMEM(((total - 16) // FOLD, LANES), f32)
    mains = pltpu.VMEM((2, nw, total, LANES), f32)
    chunks = (total - 16) // CHUNK
    return pl.pallas_call(
        functools.partial(kernel, counts),
        out_shape=(
            jax.ShapeDtypeStruct((5, 1, rows, width), f32),
            jax.ShapeDtypeStruct((2, 1, rows, width), f32),
        ),
        in_specs=[pl.BlockSpec(memory_space=pltpu.HBM)] * 2,
        out_specs=[pl.BlockSpec(memory_space=pl.ANY)] * 2,
        scratch_shapes=[plane] * 6
        + [five] * 3
        + [plane] * 8
        + [pair] * 4
        + [packet] * 9
        + [mains] * 2
        + [
            pltpu.SemaphoreType.DMA((2, nw)),
            pltpu.SemaphoreType.DMA((KINDS, nw)),
            pltpu.SemaphoreType.DMA((KINDS, nw)),
            pltpu.SemaphoreType.DMA((4, chunks)),
            pltpu.SemaphoreType.DMA((4, chunks)),
        ],
        compiler_params=pltpu.CompilerParams(
            collective_id=0, has_side_effects=True, vmem_limit_bytes=48 * 1024 * 1024
        ),
    )(*(pltpu.with_memory_space_constraint(x, pltpu.HBM) for x in (images, stiffness)))


def solution(mesh):
    counts = tuple(mesh.shape[name] for name in ("sec", "row", "col"))
    spec = P("sec", "row", "col")
    out = P(None, "sec", "row", "col")
    return jax.shard_map(
        functools.partial(local, counts), mesh=mesh, in_specs=(spec, spec),
        out_specs=(out, out), check_vma=False,
    )
```

profile of v0, /device:TPU:1, one launch (start us, length us, event | category | flops | bytes accessed | tf_op | source)
XLA Modules:
  0.0 32.0 jit_solution(11956204164261322845)
XLA Ops:
  0.6 29.5 %shard_map.41 = (f32[5,1,256,256]{3,2,1,0:T(8,128)S(1)}, f32[2,1,256,256]{3,2,1,0:T(8,128)S(1)}) custom-call(f32[1,256,256]{2,1,0:T(8,128)} %images.1, f32[1,256,256]{2,1,0:T(8,128)} %stiff.1), custom_call_target="tpu_custom_call" | custom-call | tf_op jit(solution)/shard_map/pallas_call | solution.py:518
  30.2 1.1 %copy.6 = f32[5,1,256,256]{3,2,1,0:T(8,128)} copy(f32[5,1,256,256]{3,2,1,0:T(8,128)S(1)} %get-tuple-element.4) | data formatting | bytes 2621440
  31.2 0.8 %copy.7 = f32[2,1,256,256]{3,2,1,0:T(8,128)} copy(f32[2,1,256,256]{3,2,1,0:T(8,128)S(1)} %get-tuple-element.5) | data formatting | bytes 1048576
where the time goes:
time: 32.2 us; the launch traced here: 32 us
  Pallas kernels  29.5 us (92%)
  local copies, waits for them, and re-layouts  1.85 us (6%)
  between operations  0.64 us (2%)
    pallas_call x1, Pallas kernels, local(): pl.pallas_call(functools.partial(kernel, counts), out_shape=(jax.ShapeDty...  29.5 us
    unnamed x2, local copies, waits for them, and re-layouts  1.85 us

commit v1 on v0

--- a/solution.py
+++ b/solution.py
@@ -16,6 +16,9 @@
 LANES = 128
 HALO = 16
 EDGE = HALO + 8
+GRAD = 16
+WIN = 64
+SWEEP = 32
 SLOT = 16
 CHUNK = 64
 FOLD = LANES // (2 * SLOT)
@@ -29,6 +32,10 @@
 
 def lane_roll(x, shift):
     return pltpu.roll(x, shift % x.shape[1], 1)
+
+
+def columns_of(k):
+    return slice(k * LANES, (k + 1) * LANES)
 
 
 def shifted(blocks, shift, lane):
@@ -48,9 +55,9 @@
 
 def kernel(
     counts, images, stiff, tensor_out, field_out,
-    a, b, s, q, gx, gy, pr, p3, tt, ua, ub, uc, va, vb, vc, ex, ey, g0, g1, field, last_field,
+    a, b, s, q, rq, gx, gy, pr, p3, tt, ca, cb, cc, g0, g1, g2, g3, g4, kk, field,
     send_right, send_left, got_left, got_right, next_left, next_right,
-    rim, rim_before, rim_after, main_before, main_after,
+    rim, rim_before, rim_after, main_before, main_after, band,
     local_sem, send_sem, recv_sem, chunk_send, chunk_recv,
 ):
     sec, row, col = (lax.axis_index(name) for name in ("sec", "row", "col"))
@@ -68,7 +75,7 @@
     )
     prev_id, next_id, up_id, down_id, left_id, right_id = (side[1] for side in sides)
     end = EDGE + rows
-    first, last = 8, total - 8
+    first, last = EDGE - HALO, end + HALO
     inner = pl.ds(EDGE, rows)
     main = pl.ds(0, nw)
     top, bottom = pl.ds(EDGE - HALO, HALO), pl.ds(end, HALO)
@@ -129,15 +136,6 @@
     def _():
         clear(rim_before)
         clear(main_before)
-
-    for start in (0, total - 8):
-        for ref in (a, q):
-            clear(ref.at[:, pl.ds(start, 8)])
-        for ref in (pr, p3):
-            clear(ref.at[:, :, pl.ds(start, 8)])
-    for start in (8, total - 16):
-        for ref in (g0, g1, field):
-            clear(ref.at[:, :, pl.ds(start, 8)])
 
     pl.semaphore_wait(barrier, sum(jnp.where(there, 1, 0) for there, _device in sides))
 
@@ -230,17 +228,6 @@
     unpack(a, got_left, got_right, 0)
     unpack(s, got_left, got_right, 1)
 
-    def blocks(low, high, step, body):
-        def one(i, carry):
-            body(pl.multiple_of(low + i * step, 8), step)
-            return carry
-
-        count = (high - low) // step
-        lax.fori_loop(0, count, one, 0)
-        rest = high - low - count * step
-        if rest:
-            body(low + count * step, rest)
-
     def get(ref, r, step, *lead):
         return [ref[(*lead, k, pl.ds(r, step), slice(None))] for k in range(nb)]
 
@@ -248,123 +235,137 @@
         for k, value in enumerate(values):
             ref[(*lead, k, pl.ds(r, step), slice(None))] = value
 
-    def gradient_block(r, step):
+    def blocks(low, high, step, body):
+        for r in range(low, high, step):
+            body(r, min(step, high - r))
+
+    def gradient(r, step):
         lane = lanes_of(step)
-        rr = lax.broadcasted_iota(jnp.int32, (step, LANES), 0) + r
-        row_ok = ((rr >= EDGE) | has_up) & ((rr < end) | has_down)
         rim_ok = ((lane < LANES // 2) & has_right) | ((lane >= LANES // 2) & has_left)
-        masks = [row_ok] * nw + [row_ok & rim_ok]
         mid = get(a, r, step)
         after, before = shifted(mid, -1, lane), shifted(mid, 1, lane)
         under, over = get(a, r + 1, step), get(a, r - 1, step)
-        dx = [jnp.where(m, (x - y) * 0.5, 0.0) for m, x, y in zip(masks, after, before)]
-        dy = [jnp.where(m, (x - y) * 0.5, 0.0) for m, x, y in zip(masks, under, over)]
+        dx = [x - y for x, y in zip(after, before)]
+        dy = [x - y for x, y in zip(under, over)]
+        dx[nw], dy[nw] = jnp.where(rim_ok, dx[nw], 0.0), jnp.where(rim_ok, dy[nw], 0.0)
         put(gx, dx, r, step)
         put(gy, dy, r, step)
         put(pr, [x * x for x in dx], r, step, 0)
         put(pr, [x * y for x, y in zip(dx, dy)], r, step, 1)
         put(pr, [y * y for y in dy], r, step, 2)
-        put(q, [jnp.sqrt(x) for x in get(s, r, step)], r, step)
-
-    blocks(first, last, 16, gradient_block)
-
-    def three_rows(k):
+        stiff_here = get(s, r, step)
+        inverse = [lax.rsqrt(jnp.maximum(x, 0.05)) for x in stiff_here]
+        put(rq, inverse, r, step)
+        put(q, [x * y for x, y in zip(stiff_here, inverse)], r, step)
+
+    blocks(first, last, GRAD, gradient)
+
+    for there, at in ((has_up, top), (has_down, bottom)):
+        @pl.when(jnp.logical_not(there))
+        def _():
+            for ref in (gx, gy):
+                clear(ref.at[:, at])
+            clear(pr.at[pl.ds(0, 3), :, at])
+
+    def three_rows(ks):
         def body(r, step):
-            put(p3, add(*(get(pr, r + d, step, k) for d in (-1, 0, 1))), r, step, k)
+            for k in ks:
+                put(p3, add(*(get(pr, r + d, step, k) for d in (-1, 0, 1))), r, step, k)
 
         return body
 
-    scale = jnp.where(has_next, jnp.float32(1.0), jnp.float32(0.0))
-    scale = scale * (1.0 / float((2 * RADIUS + 1) ** 2))
-
-    def window_mean(k, r, step):
-        lane = lanes_of(step)
-        summed = add(*(get(p3, r + d, step, k) for d in (-3, 0, 3)))
-        summed = add(summed, shifted(summed, 1, lane), shifted(summed, -1, lane))
-        summed = add(summed, shifted(summed, 3, lane), shifted(summed, -3, lane))
-        value = [x * scale for x in summed]
-        put(tt, value, r, step, k)
-        return value
-
-    def three_first(r, step):
-        for k in range(3):
-            three_rows(k)(r, step)
-
-    blocks(first, last, 16, three_first)
-
-    def mean_first(r, step):
-        for k in range(3):
-            window_mean(k, r, step)
-
-    blocks(16, total - 16, 16, mean_first)
+    kept = jnp.where(has_next, jnp.float32(1.0), jnp.float32(0.0))
+    cells = float((2 * RADIUS + 1) ** 2)
+
+    src = lax.broadcasted_iota(jnp.int32, (nb * LANES, nb * LANES), 0)
+    dst = lax.broadcasted_iota(jnp.int32, (nb * LANES, nb * LANES), 1)
+    fold_at = nw * LANES + LANES // 2
+    src = jnp.where(src < fold_at, src, src - nb * LANES)
+    dst = jnp.where(dst < fold_at, dst, dst - nb * LANES)
+    band[...] = jnp.where(jnp.abs(src - dst) <= RADIUS, 1.0, 0.0).astype(jnp.bfloat16)
+
+    def window(ks, factor):
+        scale = kept * (factor / cells)
+
+        def body(r, step):
+            for k in ks:
+                x = jnp.concatenate(add(*(get(p3, r + d, step, k) for d in (-3, 0, 3))), axis=1)
+                coarse = x.astype(jnp.bfloat16)
+                fine = (x - coarse.astype(jnp.float32)).astype(jnp.bfloat16)
+                both = jnp.concatenate([coarse, fine], axis=0)
+                y = jnp.dot(both, band[...], preferred_element_type=jnp.float32)
+                y = (y[:step] + y[step:]) * scale
+                value = [y[:, columns_of(j)] for j in range(nb)]
+                put(tt, value, r, step, k)
+                if EDGE <= r < end:
+                    for j in range(nw):
+                        tensor_out[k, 0, pl.ds(r - EDGE, step), columns(j)] = value[j]
+
+        body(first, 16)
+        blocks(EDGE, end, WIN, body)
+        body(end, 16)
+
+    blocks(first, last, 16, three_rows((0, 1, 2)))
+    window((0, 1, 2), 0.25)
 
     when_got(has_next, tile_b + forward_rows + forward_cols)
     unpack(b, next_left, next_right, 0)
 
-    def change_block(r, step):
-        change = [x - y for x, y in zip(get(b, r, step), get(a, r, step))]
-        put(pr, [x * y for x, y in zip(get(gx, r, step), change)], r, step, 3)
-        put(pr, [x * y for x, y in zip(get(gy, r, step), change)], r, step, 4)
-
-    blocks(first, last, 32, change_block)
-
-    def three_second(r, step):
-        for k in (3, 4):
-            three_rows(k)(r, step)
-
-    blocks(first, last, 16, three_second)
-
-    def tensor_block(r, step):
+    def change(r, step):
+        moved = [x - y for x, y in zip(get(b, r, step), get(a, r, step))]
+        put(pr, [x * y for x, y in zip(get(gx, r, step), moved)], r, step, 3)
+        put(pr, [x * y for x, y in zip(get(gy, r, step), moved)], r, step, 4)
+
+    blocks(first, last, 32, change)
+    blocks(first, last, 16, three_rows((3, 4)))
+    window((3, 4), 0.5)
+
+    def near(source, r, step, part, count):
+        mid = get(source, r, step, part)
         lane = lanes_of(step)
-        parts = [get(tt, r, step, k) for k in range(3)]
-        parts += [window_mean(k, r, step) for k in (3, 4)]
+        return add(
+            get(source, r - 1, step, part), get(source, r + 1, step, part),
+            shifted(mid, 1, lane), shifted(mid, -1, lane),
+        )[:count]
+
+    def relaxed(source, r, step, start, count):
+        nx, ny = (near(source, r, step, part, count) for part in range(2))
+        xx, xy, yy = (get(ref, r, step)[:count] for ref in (ca, cb, cc))
+        x, y = start
+        return (
+            [x[k] + (xx[k] * nx[k] - xy[k] * ny[k]) for k in range(count)],
+            [y[k] + (yy[k] * ny[k] - xy[k] * nx[k]) for k in range(count)],
+        )
+
+    def setup(r, step):
+        lane = lanes_of(step)
+        xx, xy, yy, xt, yt = (get(tt, r, step, k) for k in range(5))
         mid = get(q, r, step)
         around = add(
             get(q, r - 1, step), get(q, r + 1, step), shifted(mid, 1, lane), shifted(mid, -1, lane)
         )
+        at = pl.ds(r, step)
         for k in range(nb):
-            xx, xy, yy, xt, yt = (part[k] for part in parts)
             diag = mid[k] * around[k] + 2.0 * COUPLING
-            one, two = xx + diag, yy + diag
-            inverse = 1.0 / (one * two - xy * xy)
-            ca, cb, cc = two * inverse, xy * inverse, one * inverse
-            x, y = cb * yt - ca * xt, cb * xt - cc * yt
-            at = pl.ds(r, step)
-            for ref, value in ((va, ca), (vb, cb), (vc, cc)):
-                ref[k, at, :] = value * COUPLING
-            for ref, value in ((ua, ca), (ub, cb), (uc, cc)):
+            one, two = xx[k] + diag, yy[k] + diag
+            inverse = mid[k] / (one * two - xy[k] * xy[k])
+            xa, xb, xc = two * inverse, xy[k] * inverse, one * inverse
+            g0[0, k, at, :] = xb * yt[k] - xa * xt[k]
+            g0[1, k, at, :] = xb * xt[k] - xc * yt[k]
+            for ref, value in ((ca, xa), (cb, xb), (cc, xc)):
                 ref[k, at, :] = value * mid[k]
-            ex[k, at, :] = x
-            ey[k, at, :] = y
-            g0[0, k, at, :] = x * mid[k]
-            g0[1, k, at, :] = y * mid[k]
-
-    def relaxed(source, r, step, x, y):
-        lane = lanes_of(step)
-
-        def near(part):
-            mid = get(source, r, step, part)
-            return add(
-                get(source, r - 1, step, part), get(source, r + 1, step, part),
-                shifted(mid, 1, lane), shifted(mid, -1, lane),
+
+    def sweep(source, start, target, unscaled=None):
+        def body(r, step):
+            new = relaxed(
+                source, r, step, [get(start, r, step, part) for part in range(2)], nb
             )
-
-        nx, ny = near(0), near(1)
-        ca, cb, cc = (get(ref, r, step) for ref in (ua, ub, uc))
-        return (
-            [x[k] + ca[k] * nx[k] - cb[k] * ny[k] for k in range(nb)],
-            [y[k] + cc[k] * ny[k] - cb[k] * nx[k] for k in range(nb)],
-        )
-
-    def sweep(source, target, scaled=None):
-        def body(r, step):
-            new = relaxed(source, r, step, get(ex, r, step), get(ey, r, step))
-            mid = get(q, r, step) if scaled is not None else None
+            here = get(rq, r, step) if unscaled is not None else None
             for part in range(2):
                 if target is not None:
                     put(target, new[part], r, step, part)
-                if scaled is not None:
-                    put(scaled, [m * x for m, x in zip(mid, new[part])], r, step, part)
+                if unscaled is not None:
+                    put(unscaled, [x * y for x, y in zip(new[part], here)], r, step, part)
 
         return body
 
@@ -377,13 +378,9 @@
             margin = ends[k == len(bodies) - 1]
             low = first + margin if c == 0 else bounds[c] + ahead
             high = last - margin if c == chunks - 1 else bounds[c + 1] + ahead
-            blocks(low, high, 32, body)
-
-    first_round = [tensor_block]
-    now, other = g0, g1
-    for k in range(1, SWEEPS):
-        first_round.append(sweep(now, field if k == SWEEPS - 1 else None, other))
-        now, other = other, now
+            blocks(low, high, SWEEP, body)
+
+    first_round = [setup, sweep(g0, g0, g1), sweep(g1, g0, g2), sweep(g2, g0, g3, field)]
 
     to_next, to_prev = [], []
     for c in range(chunks):
@@ -391,7 +388,7 @@
         low, high = bounds[c], bounds[c + 1]
         folded = pl.ds((low - first) // FOLD, (high - low) // FOLD)
         pack_rim(field, rim, low, high, first, nw)
-        rows_sent = pl.ds(max(low, 16), min(high, total - 16) - max(low, 16))
+        rows_sent = pl.ds(max(low, first + 8), min(high, last - 8) - max(low, first + 8))
 
         def moves(rims, mains, device, way):
             pairs = (
@@ -411,17 +408,7 @@
         when_start(has_next, to_next[c])
         when_start(has_prev, to_prev[c])
 
-    put_tensor = [
-        pltpu.make_async_copy(
-            tt.at[:, k, inner], tensor_out.at[:, 0, :, columns(k)], local_sem.at[0, k]
-        )
-        for k in range(nw)
-    ]
-    for copy in put_tensor:
-        copy.start()
-
-
-    def first_block(r, step):
+    def coupled(r, step):
         at = pl.ds(r, step)
 
         def beside(part, ref):
@@ -430,25 +417,27 @@
             ] + [ref[nw, at, :]]
 
         x, y = beside(0, gx), beside(1, gy)
-        ca, cb, cc = (get(ref, r, step) for ref in (va, vb, vc))
-        old_x, old_y = get(ex, r, step), get(ey, r, step)
-        new_x = [old_x[k] + ca[k] * x[k] - cb[k] * y[k] for k in range(nb)]
-        new_y = [old_y[k] + cc[k] * y[k] - cb[k] * x[k] for k in range(nb)]
-        put(ex, new_x, r, step)
-        put(ey, new_y, r, step)
-        mid = get(q, r, step)
-        for part, values in enumerate(relaxed(now, r, step, new_x, new_y)):
-            put(other, [m * v for m, v in zip(mid, values)], r, step, part)
-
-    second_round = [first_block]
-    source, target = other, now
-    for k in range(1, SWEEPS):
-        if k == SWEEPS - 1:
-            second_round.append(sweep(source, last_field))
-        else:
-            second_round.append(sweep(source, None, target))
-        source, target = target, source
-
+        xx, xy, yy = (get(ref, r, step) for ref in (ca, cb, cc))
+        weight = [v * COUPLING for v in get(rq, r, step)]
+        old = [get(g0, r, step, part) for part in range(2)]
+        start = (
+            [old[0][k] + weight[k] * (xx[k] * x[k] - xy[k] * y[k]) for k in range(nb)],
+            [old[1][k] + weight[k] * (yy[k] * y[k] - xy[k] * x[k]) for k in range(nb)],
+        )
+        new = relaxed(g3, r, step, start, nb)
+        for part in range(2):
+            put(kk, start[part], r, step, part)
+            put(g1, new[part], r, step, part)
+
+    def final(r, step):
+        start = [get(kk, r, step, part) for part in range(2)]
+        new = relaxed(g4, r, step, start, nw)
+        here = get(rq, r, step)
+        for part in range(2):
+            for k in range(nw):
+                field_out[part, 0, pl.ds(r - EDGE, step), columns(k)] = new[part][k] * here[k]
+
+    second_round = [coupled, sweep(g1, kk, g2), sweep(g2, kk, g4), final]
     for c in range(chunks):
         when_got(has_prev, to_next[c])
         when_got(has_next, to_prev[c])
@@ -470,22 +459,11 @@
     for c in range(chunks):
         when_sent(has_next, to_next[c])
         when_sent(has_prev, to_prev[c])
-
-    put_field = [
-        pltpu.make_async_copy(
-            last_field.at[:, k, inner], field_out.at[:, 0, :, columns(k)], local_sem.at[1, k]
-        )
-        for k in range(nw)
-    ]
-    for copy in put_field:
-        copy.start()
     when_sent(has_up, up)
     when_sent(has_down, down)
     when_sent(has_right, [col_right])
     when_sent(has_left, [col_left])
     when_sent(has_prev, tile_b + forward_rows + forward_cols)
-    for copy in put_tensor + put_field:
-        copy.wait()
 
 
 def pack_rim(field, rim, low, high, first, nw):
@@ -512,9 +490,9 @@
     plane = pltpu.VMEM((nb, total, LANES), f32)
     five = pltpu.VMEM((5, nb, total, LANES), f32)
     pair = pltpu.VMEM((2, nb, total, LANES), f32)
-    packet = pltpu.VMEM(((total - 16) // FOLD, LANES), f32)
+    packet = pltpu.VMEM(((rows + 2 * HALO) // FOLD, LANES), f32)
     mains = pltpu.VMEM((2, nw, total, LANES), f32)
-    chunks = (total - 16) // CHUNK
+    chunks = (rows + 2 * HALO) // CHUNK
     return pl.pallas_call(
         functools.partial(kernel, counts),
         out_shape=(
@@ -522,13 +500,14 @@
             jax.ShapeDtypeStruct((2, 1, rows, width), f32),
         ),
         in_specs=[pl.BlockSpec(memory_space=pltpu.HBM)] * 2,
-        out_specs=[pl.BlockSpec(memory_space=pl.ANY)] * 2,
-        scratch_shapes=[plane] * 6
+        out_specs=[pl.BlockSpec(memory_space=pltpu.VMEM)] * 2,
+        scratch_shapes=[plane] * 7
         + [five] * 3
-        + [plane] * 8
-        + [pair] * 4
+        + [plane] * 3
+        + [pair] * 7
         + [packet] * 9
         + [mains] * 2
+        + [pltpu.VMEM((nb * LANES, nb * LANES), jnp.bfloat16)]
         + [
             pltpu.SemaphoreType.DMA((2, nw)),
             pltpu.SemaphoreType.DMA((KINDS, nw)),

time: 32.2 us -> 26.3 us (0.82)
  Pallas kernels: 29.5 us -> 23.6 us
    pallas_call x1, Pallas kernels: 29.5 us -> 23.6 us  [local(): pl.pallas_call(functools.partial(kernel, counts), out_shape=(jax.ShapeDty...]
where the time goes in v1:
time: 26.3 us; the launch traced here: 26.1 us
  Pallas kernels  23.6 us (90%)
  local copies, waits for them, and re-layouts  1.85 us (7%)
  between operations  0.64 us (2%)
    pallas_call x1, Pallas kernels, local(): pl.pallas_call(functools.partial(kernel, counts), out_shape=(jax.ShapeDty...  23.6 us
    unnamed x2, local copies, waits for them, and re-layouts  1.85 us

profile of v1, /device:TPU:1, one launch (start us, length us, event | category | flops | bytes accessed | tf_op | source)
XLA Modules:
  0.0 26.1 jit_solution(4247555755719050153)
XLA Ops:
  0.6 23.6 %shard_map.41 = (f32[5,1,256,256]{3,2,1,0:T(8,128)S(1)}, f32[2,1,256,256]{3,2,1,0:T(8,128)S(1)}) custom-call(f32[1,256,256]{2,1,0:T(8,128)} %images.1, f32[1,256,256]{2,1,0:T(8,128)} %stiff.1), custom_call_target="tpu_custom_call" | custom-call | tf_op jit(solution)/shard_map/pallas_call | solution.py:496
  24.3 1.1 %copy.6 = f32[5,1,256,256]{3,2,1,0:T(8,128)} copy(f32[5,1,256,256]{3,2,1,0:T(8,128)S(1)} %get-tuple-element.4) | data formatting | bytes 2621440
  25.3 0.8 %copy.7 = f32[2,1,256,256]{3,2,1,0:T(8,128)} copy(f32[2,1,256,256]{3,2,1,0:T(8,128)S(1)} %get-tuple-element.5) | data formatting | bytes 1048576

commit v2 on v1

--- a/solution.py
+++ b/solution.py
@@ -19,6 +19,7 @@
 GRAD = 16
 WIN = 64
 SWEEP = 32
+EARLY = 2
 SLOT = 16
 CHUNK = 64
 FOLD = LANES // (2 * SLOT)
@@ -58,7 +59,7 @@
     a, b, s, q, rq, gx, gy, pr, p3, tt, ca, cb, cc, g0, g1, g2, g3, g4, kk, field,
     send_right, send_left, got_left, got_right, next_left, next_right,
     rim, rim_before, rim_after, main_before, main_after, band,
-    local_sem, send_sem, recv_sem, chunk_send, chunk_recv,
+    local_sem, send_sem, recv_sem, chunk_send, chunk_recv, tile_send, tile_recv,
 ):
     sec, row, col = (lax.axis_index(name) for name in ("sec", "row", "col"))
     n_sec, n_row, n_col = counts
@@ -145,7 +146,23 @@
         ]
 
     low, high = pl.ds(0, HALO), pl.ds(rows - HALO, HALO)
-    tile_b = by_block(images, pl.ds(0, rows), b, inner, TILE_B, prev_id)
+    bounds = list(range(first, last - CHUNK + 1, CHUNK)) + [last]
+    chunks = len(bounds) - 1
+    ahead = 8 * (SWEEPS + 1)
+    cuts = [0] + [min(high + ahead - EDGE, rows) for high in bounds[1:-1]] + [rows]
+
+    def tile_piece(c):
+        at, to = pl.ds(cuts[c], cuts[c + 1] - cuts[c]), pl.ds(EDGE + cuts[c], cuts[c + 1] - cuts[c])
+        return [
+            pltpu.make_async_remote_copy(
+                src_ref=images.at[0, at, columns(p)], dst_ref=b.at[p, to],
+                send_sem=tile_send.at[c, p], recv_sem=tile_recv.at[c, p],
+                device_id=prev_id, device_id_type=MESH,
+            )
+            for p in range(nw)
+        ]
+
+    tile_b = [tile_piece(c) for c in range(chunks)]
     up = by_block(stiff, low, s, bottom, ROW_S_UP, up_id)
     up += by_block(images, low, a, bottom, ROW_A_UP, up_id)
     down = by_block(stiff, high, s, top, ROW_S_DOWN, down_id)
@@ -181,12 +198,12 @@
 
     when_start(has_up, up)
     when_start(has_down, down)
-    when_start(has_prev, tile_b)
+    when_start(has_prev, sum(tile_b[:EARLY], []))
     for copy in loads:
         copy.wait()
     when_got(has_up, down)
     when_got(has_down, up)
-    when_start(has_prev, forward_rows)
+    when_start(has_prev, forward_rows + sum(tile_b[EARLY:EARLY + 1], []))
 
     def lanes_of(count):
         return lax.broadcasted_iota(jnp.int32, (count, LANES), 1)
@@ -224,7 +241,7 @@
 
     when_got(has_left, [col_right])
     when_got(has_right, [col_left])
-    when_start(has_prev, forward_cols)
+    when_start(has_prev, forward_cols + sum(tile_b[EARLY + 1:], []))
     unpack(a, got_left, got_right, 0)
     unpack(s, got_left, got_right, 1)
 
@@ -284,7 +301,7 @@
     dst = jnp.where(dst < fold_at, dst, dst - nb * LANES)
     band[...] = jnp.where(jnp.abs(src - dst) <= RADIUS, 1.0, 0.0).astype(jnp.bfloat16)
 
-    def window(ks, factor):
+    def window(low, high, ks, factor):
         scale = kept * (factor / cells)
 
         def body(r, step):
@@ -301,24 +318,20 @@
                     for j in range(nw):
                         tensor_out[k, 0, pl.ds(r - EDGE, step), columns(j)] = value[j]
 
-        body(first, 16)
-        blocks(EDGE, end, WIN, body)
-        body(end, 16)
+        if low < EDGE:
+            body(low, EDGE - low)
+        blocks(max(low, EDGE), min(high, end), WIN, body)
+        if high > end:
+            body(end, high - end)
 
     blocks(first, last, 16, three_rows((0, 1, 2)))
-    window((0, 1, 2), 0.25)
-
-    when_got(has_next, tile_b + forward_rows + forward_cols)
-    unpack(b, next_left, next_right, 0)
+    window(first + 8, last - 8, (0, 1, 2), 0.25)
+
 
     def change(r, step):
         moved = [x - y for x, y in zip(get(b, r, step), get(a, r, step))]
         put(pr, [x * y for x, y in zip(get(gx, r, step), moved)], r, step, 3)
         put(pr, [x * y for x, y in zip(get(gy, r, step), moved)], r, step, 4)
-
-    blocks(first, last, 32, change)
-    blocks(first, last, 16, three_rows((3, 4)))
-    window((3, 4), 0.5)
 
     def near(source, r, step, part, count):
         mid = get(source, r, step, part)
@@ -369,21 +382,27 @@
 
         return body
 
-    bounds = list(range(first, last - CHUNK + 1, CHUNK)) + [last]
-    chunks = len(bounds) - 1
+    def span(c, ahead, margin):
+        low = first + margin if c == 0 else bounds[c] + ahead
+        high = last - margin if c == chunks - 1 else bounds[c + 1] + ahead
+        return low, high
 
     def stages(c, bodies, lead, ends):
         for k, body in enumerate(bodies):
-            ahead = 8 * (lead - k)
-            margin = ends[k == len(bodies) - 1]
-            low = first + margin if c == 0 else bounds[c] + ahead
-            high = last - margin if c == chunks - 1 else bounds[c + 1] + ahead
-            blocks(low, high, SWEEP, body)
+            blocks(*span(c, 8 * (lead - k), ends[k == len(bodies) - 1]), SWEEP, body)
 
     first_round = [setup, sweep(g0, g0, g1), sweep(g1, g0, g2), sweep(g2, g0, g3, field)]
 
     to_next, to_prev = [], []
     for c in range(chunks):
+        when_got(has_next, tile_b[c])
+        if c == 0:
+            when_got(has_next, forward_rows + forward_cols)
+            unpack(b, next_left, next_right, 0)
+        settled = 8 * (SWEEPS - 1)
+        blocks(*span(c, settled + 16, 0), 32, change)
+        blocks(*span(c, settled + 8, 0), 16, three_rows((3, 4)))
+        window(*span(c, settled, 8), (3, 4), 0.5)
         stages(c, first_round, SWEEPS - 1, (8, 8))
         low, high = bounds[c], bounds[c + 1]
         folded = pl.ds((low - first) // FOLD, (high - low) // FOLD)
@@ -463,7 +482,7 @@
     when_sent(has_down, down)
     when_sent(has_right, [col_right])
     when_sent(has_left, [col_left])
-    when_sent(has_prev, tile_b + forward_rows + forward_cols)
+    when_sent(has_prev, sum(tile_b, []) + forward_rows + forward_cols)
 
 
 def pack_rim(field, rim, low, high, first, nw):
@@ -481,6 +500,19 @@
     rim[pl.ds((low - first) // FOLD, size), :] = out
 
 
+def store(tensor, field, tensor_out, field_out, sem):
+    pairs = ((tensor, tensor_out), (field, field_out))
+    copies = [
+        pltpu.make_async_copy(src.at[k], dst.at[k], sem.at[i, k])
+        for i, (src, dst) in enumerate(pairs)
+        for k in range(src.shape[0])
+    ]
+    for copy in copies:
+        copy.start()
+    for copy in copies:
+        copy.wait()
+
+
 def local(counts, images, stiffness):
     _, rows, width = images.shape
     nw = width // LANES
@@ -493,7 +525,7 @@
     packet = pltpu.VMEM(((rows + 2 * HALO) // FOLD, LANES), f32)
     mains = pltpu.VMEM((2, nw, total, LANES), f32)
     chunks = (rows + 2 * HALO) // CHUNK
-    return pl.pallas_call(
+    results = pl.pallas_call(
         functools.partial(kernel, counts),
         out_shape=(
             jax.ShapeDtypeStruct((5, 1, rows, width), f32),
@@ -514,11 +546,21 @@
             pltpu.SemaphoreType.DMA((KINDS, nw)),
             pltpu.SemaphoreType.DMA((4, chunks)),
             pltpu.SemaphoreType.DMA((4, chunks)),
+            pltpu.SemaphoreType.DMA((chunks, nw)),
+            pltpu.SemaphoreType.DMA((chunks, nw)),
         ],
         compiler_params=pltpu.CompilerParams(
             collective_id=0, has_side_effects=True, vmem_limit_bytes=48 * 1024 * 1024
         ),
     )(*(pltpu.with_memory_space_constraint(x, pltpu.HBM) for x in (images, stiffness)))
+    return pl.pallas_call(
+        store,
+        out_shape=tuple(jax.ShapeDtypeStruct(x.shape, f32) for x in results),
+        in_specs=[pl.BlockSpec(memory_space=pltpu.VMEM)] * 2,
+        out_specs=[pl.BlockSpec(memory_space=pltpu.HBM)] * 2,
+        scratch_shapes=[pltpu.SemaphoreType.DMA((2, 5))],
+        compiler_params=pltpu.CompilerParams(vmem_limit_bytes=4 * 1024 * 1024),
+    )(*results)
 
 
 def solution(mesh):

time: 26.3 us -> 25.6 us (0.973)
  local copies, waits for them, and re-layouts: 1.85 us -> 0 us
  Pallas kernels: 23.6 us -> 24.8 us
    unnamed x2 -> x0, local copies, waits for them, and re-layouts: 1.85 us -> none
    pallas_call x0 -> x1, Pallas kernels: none -> 1.31 us  [local(): pl.pallas_call(store, out_shape=tuple((jax.ShapeDtypeStruct(x.shape, f32)...]
where the time goes in v2:
time: 25.6 us; the launch traced here: 25.5 us
  Pallas kernels  24.8 us (97%)
  between operations  0.64 us (2%)
    pallas_call x1, Pallas kernels, local(): pl.pallas_call(functools.partial(kernel, counts), out_shape=(jax.ShapeDty...  23.5 us
    pallas_call x1, Pallas kernels, local(): pl.pallas_call(store, out_shape=tuple((jax.ShapeDtypeStruct(x.shape, f32)...  1.31 us

profile of v2, /device:TPU:1, one launch (start us, length us, event | category | flops | bytes accessed | tf_op | source)
XLA Modules:
  0.0 25.5 jit_solution(2534803187957501817)
XLA Ops:
  0.6 23.5 %shard_map.41 = (f32[5,1,256,256]{3,2,1,0:T(8,128)S(1)}, f32[2,1,256,256]{3,2,1,0:T(8,128)S(1)}) custom-call(f32[1,256,256]{2,1,0:T(8,128)} %images.1, f32[1,256,256]{2,1,0:T(8,128)} %stiff.1), custom_call_target="tpu_custom_call" | custom-call | tf_op jit(solution)/shard_map/pallas_call | solution.py:528
  24.1 1.3 %shard_map.42 = (f32[5,1,256,256]{3,2,1,0:T(8,128)}, f32[2,1,256,256]{3,2,1,0:T(8,128)}) custom-call(f32[5,1,256,256]{3,2,1,0:T(8,128)S(1)} %get-tuple-element.4.tensor, f32[2,1,256,256]{3,2,1,0:T(8,128)S(1)} %get-tuple-element.5.field), custom_call_target="tpu_custom_call" | custom-call | tf_op jit(solution)/shard_map/pallas_call | solution.py:556

commit v3 on v2

--- a/solution.py
+++ b/solution.py
@@ -16,19 +16,27 @@
 LANES = 128
 HALO = 16
 EDGE = HALO + 8
+LEAD = 9
 GRAD = 16
 WIN = 64
 SWEEP = 32
 EARLY = 2
 SLOT = 16
 CHUNK = 64
+SHORT = 32
 FOLD = LANES // (2 * SLOT)
 
 (
     TILE_B, ROW_A_UP, ROW_A_DOWN, ROW_S_UP, ROW_S_DOWN, FWD_TOP, FWD_BOTTOM, COL_RIGHT, COL_LEFT,
-    FWD_RIGHT, FWD_LEFT,
-) = range(11)
-KINDS = 11
+    FWD_RIGHT, FWD_LEFT, CORNER, _, _, _, FWD_CORNER, _, _, _,
+) = range(19)
+KINDS = 19
+
+
+def bounds_of(rows, first):
+    last = first + rows + 2 * HALO
+    inside = list(range(first + SHORT, last - SHORT - CHUNK // 2, CHUNK))
+    return [first] + inside + [last - SHORT, last]
 
 
 def lane_roll(x, shift):
@@ -57,7 +65,7 @@
 def kernel(
     counts, images, stiff, tensor_out, field_out,
     a, b, s, q, rq, gx, gy, pr, p3, tt, ca, cb, cc, g0, g1, g2, g3, g4, kk, field,
-    send_right, send_left, got_left, got_right, next_left, next_right,
+    send_right, send_left, got_left, got_right, next_left, next_right, corner, next_corner,
     rim, rim_before, rim_after, main_before, main_after, band,
     local_sem, send_sem, recv_sem, chunk_send, chunk_recv, tile_send, tile_recv,
 ):
@@ -75,6 +83,11 @@
         (has_left, (sec, row, col - 1)), (has_right, (sec, row, col + 1)),
     )
     prev_id, next_id, up_id, down_id, left_id, right_id = (side[1] for side in sides)
+    corners = tuple(
+        (there_row & there_col, (sec, row + step_row, col + step_col))
+        for there_row, step_row in ((has_up, -1), (has_down, 1))
+        for there_col, step_col in ((has_left, -1), (has_right, 1))
+    )
     end = EDGE + rows
     first, last = EDGE - HALO, end + HALO
     inner = pl.ds(EDGE, rows)
@@ -99,7 +112,7 @@
     for copy in loads:
         copy.start()
     barrier = pltpu.get_barrier_semaphore()
-    for there, device in sides:
+    for there, device in sides + corners:
         @pl.when(there)
         def _():
             pl.semaphore_signal(barrier, inc=1, device_id=device, device_id_type=MESH)
@@ -110,24 +123,35 @@
     @pl.when(jnp.logical_not(has_up))
     def _():
         clear(a.at[main, top])
+        clear(b.at[main, top])
         clear(s.at[main, top])
 
     @pl.when(jnp.logical_not(has_down))
     def _():
         clear(a.at[main, bottom])
+        clear(b.at[main, bottom])
         clear(s.at[main, bottom])
 
     @pl.when(jnp.logical_not(has_left))
     def _():
         clear(got_left)
+        clear(next_left)
 
     @pl.when(jnp.logical_not(has_right))
     def _():
         clear(got_right)
+        clear(next_right)
+
+    for i, (there, _device) in enumerate(corners):
+        @pl.when(jnp.logical_not(there))
+        def _():
+            clear(corner.at[i])
+            clear(next_corner.at[i])
 
     @pl.when(jnp.logical_not(has_next))
     def _():
         clear(b)
+        clear(next_corner)
         clear(next_left)
         clear(next_right)
         clear(rim_after)
@@ -138,7 +162,14 @@
         clear(rim_before)
         clear(main_before)
 
-    pl.semaphore_wait(barrier, sum(jnp.where(there, 1, 0) for there, _device in sides))
+    src = lax.broadcasted_iota(jnp.int32, (nb * LANES, nb * LANES), 0)
+    dst = lax.broadcasted_iota(jnp.int32, (nb * LANES, nb * LANES), 1)
+    fold_at = nw * LANES + LANES // 2
+    src = jnp.where(src < fold_at, src, src - nb * LANES)
+    dst = jnp.where(dst < fold_at, dst, dst - nb * LANES)
+    band[...] = jnp.where(jnp.abs(src - dst) <= RADIUS, 1.0, 0.0).astype(jnp.bfloat16)
+
+    pl.semaphore_wait(barrier, sum(jnp.where(there, 1, 0) for there, _device in sides + corners))
 
     def by_block(src, at, dst, to, k, device):
         return [
@@ -146,12 +177,14 @@
         ]
 
     low, high = pl.ds(0, HALO), pl.ds(rows - HALO, HALO)
-    bounds = list(range(first, last - CHUNK + 1, CHUNK)) + [last]
+    bounds = bounds_of(rows, first)
     chunks = len(bounds) - 1
     ahead = 8 * (SWEEPS + 1)
     cuts = [0] + [min(high + ahead - EDGE, rows) for high in bounds[1:-1]] + [rows]
 
     def tile_piece(c):
+        if cuts[c] == cuts[c + 1]:
+            return []
         at, to = pl.ds(cuts[c], cuts[c + 1] - cuts[c]), pl.ds(EDGE + cuts[c], cuts[c + 1] - cuts[c])
         return [
             pltpu.make_async_remote_copy(
@@ -170,12 +203,22 @@
     col_right = remote(send_right, got_left, COL_RIGHT, right_id)
     col_left = remote(send_left, got_right, COL_LEFT, left_id)
     forward_rows = [
-        remote(a.at[main, top], b.at[main, top], FWD_TOP, prev_id),
-        remote(a.at[main, bottom], b.at[main, bottom], FWD_BOTTOM, prev_id),
+        (has_up, remote(a.at[main, top], b.at[main, top], FWD_TOP, prev_id)),
+        (has_down, remote(a.at[main, bottom], b.at[main, bottom], FWD_BOTTOM, prev_id)),
     ]
     forward_cols = [
-        remote(got_left, next_left, FWD_LEFT, prev_id),
-        remote(got_right, next_right, FWD_RIGHT, prev_id),
+        (has_left, remote(got_left, next_left, FWD_LEFT, prev_id)),
+        (has_right, remote(got_right, next_right, FWD_RIGHT, prev_id)),
+    ] + [
+        (there, remote(corner.at[i], next_corner.at[i], FWD_CORNER + i, prev_id))
+        for i, (there, _device) in enumerate(corners)
+    ]
+    head, tail = pl.ds(HALO, HALO), pl.ds(piece - 2 * HALO, HALO)
+    to_corner = [
+        remote(sent.at[at], corner.at[3 - i], CORNER + i, corners[i][1])
+        for i, (sent, at) in enumerate(
+            ((send_left, head), (send_right, head), (send_left, tail), (send_right, tail))
+        )
     ]
 
     def when_start(there, copies):
@@ -201,49 +244,67 @@
     when_start(has_prev, sum(tile_b[:EARLY], []))
     for copy in loads:
         copy.wait()
+    def lanes_of(count):
+        return lax.broadcasted_iota(jnp.int32, (count, LANES), 1)
+
+    def packed(to, block, at):
+        for low, high, folds in (
+            (0, HALO, range(1, FOLD)), (HALO, piece - HALO, range(FOLD)),
+            (piece - HALO, piece, range(FOLD - 1)),
+        ):
+            lane = lanes_of(high - low)
+            out = jnp.zeros((high - low, LANES), jnp.float32)
+            for j in folds:
+                span = pl.ds(first + j * piece + low, high - low)
+                for k, ref in enumerate((a, s)):
+                    slot = (2 * j + k) * SLOT
+                    moved = lane_roll(ref[block, span, :], slot - at)
+                    out = jnp.where((lane >= slot) & (lane < slot + SLOT), moved, out)
+            to[pl.ds(low, high - low), :] = out
+
+    def rim_of(left, right, j, k):
+        lane = lanes_of(right.shape[0])
+        slot = (2 * j + k) * SLOT
+        from_right = jnp.where(lane < SLOT, lane_roll(right, -slot), 0.0)
+        return jnp.where(lane >= LANES - SLOT, lane_roll(left, LANES - SLOT - slot), from_right)
+
+    def unpack(ref, left, right, around, k):
+        for j in range(FOLD):
+            low = HALO if j == 0 else 0
+            high = piece - HALO if j == FOLD - 1 else piece
+            at = pl.ds(low, high - low)
+            ref[nw, pl.ds(first + j * piece + low, high - low), :] = rim_of(
+                left[at, :], right[at, :], j, k
+            )
+        ref[nw, top, :] = rim_of(around[0], around[1], FOLD - 1, k)
+        ref[nw, bottom, :] = rim_of(around[2], around[3], 0, k)
+
+    @pl.when(has_right)
+    def _():
+        packed(send_right, nw - 1, LANES - SLOT)
+        col_right.start()
+
+    @pl.when(has_left)
+    def _():
+        packed(send_left, 0, 0)
+        col_left.start()
+
+    for (there, _device), copy in zip(corners, to_corner):
+        when_start(there, [copy])
     when_got(has_up, down)
     when_got(has_down, up)
-    when_start(has_prev, forward_rows + sum(tile_b[EARLY:EARLY + 1], []))
-
-    def lanes_of(count):
-        return lax.broadcasted_iota(jnp.int32, (count, LANES), 1)
-
-    lane = lanes_of(piece)
-
-    def packed(block, at):
-        out = jnp.zeros((piece, LANES), jnp.float32)
-        for j in range(FOLD):
-            span = pl.ds(first + j * piece, piece)
-            for k, ref in enumerate((a, s)):
-                low = (2 * j + k) * SLOT
-                moved = lane_roll(ref[block, span, :], low - at)
-                out = jnp.where((lane >= low) & (lane < low + SLOT), moved, out)
-        return out
-
-    def unpack(ref, left, right, k):
-        for j in range(FOLD):
-            low = (2 * j + k) * SLOT
-            from_right = jnp.where(lane < SLOT, lane_roll(right[...], -low), 0.0)
-            from_left = lane_roll(left[...], LANES - SLOT - low)
-            ref[nw, pl.ds(first + j * piece, piece), :] = jnp.where(
-                lane >= LANES - SLOT, from_left, from_right
-            )
-
-    @pl.when(has_right)
-    def _():
-        send_right[...] = packed(nw - 1, LANES - SLOT)
-        col_right.start()
-
-    @pl.when(has_left)
-    def _():
-        send_left[...] = packed(0, 0)
-        col_left.start()
-
+    for there, copy in forward_rows:
+        when_start(has_prev & there, [copy])
+    when_start(has_prev, sum(tile_b[EARLY:EARLY + 1], []))
     when_got(has_left, [col_right])
     when_got(has_right, [col_left])
-    when_start(has_prev, forward_cols + sum(tile_b[EARLY + 1:], []))
-    unpack(a, got_left, got_right, 0)
-    unpack(s, got_left, got_right, 1)
+    for (there, _device), copy in zip(corners, reversed(to_corner)):
+        when_got(there, [copy])
+    for there, copy in forward_cols:
+        when_start(has_prev & there, [copy])
+    when_start(has_prev, sum(tile_b[EARLY + 1:], []))
+    unpack(a, got_left, got_right, corner, 0)
+    unpack(s, got_left, got_right, corner, 1)
 
     def get(ref, r, step, *lead):
         return [ref[(*lead, k, pl.ds(r, step), slice(None))] for k in range(nb)]
@@ -275,58 +336,66 @@
         put(rq, inverse, r, step)
         put(q, [x * y for x, y in zip(stiff_here, inverse)], r, step)
 
-    blocks(first, last, GRAD, gradient)
-
-    for there, at in ((has_up, top), (has_down, bottom)):
+    def three_rows(ks):
+        def body(r, step):
+            for k in ks:
+                put(p3, add(*(get(pr, r + d, step, k) for d in (-1, 0, 1))), r, step, k)
+
+        return body
+
+    kept = jnp.where(has_next, jnp.float32(1.0), jnp.float32(0.0))
+    cells = float((2 * RADIUS + 1) ** 2)
+
+    def window(low, high, ks, factor):
+        scale = kept * (factor / cells)
+
+        def body(r, step):
+            parts = []
+            for k in ks:
+                x = jnp.concatenate(add(*(get(p3, r + d, step, k) for d in (-3, 0, 3))), axis=1)
+                coarse = x.astype(jnp.bfloat16)
+                parts += [coarse, (x - coarse.astype(jnp.float32)).astype(jnp.bfloat16)]
+            y = jnp.dot(
+                jnp.concatenate(parts, axis=0), band[...], preferred_element_type=jnp.float32
+            )
+            for i, k in enumerate(ks):
+                z = y[2 * i * step:(2 * i + 1) * step] + y[(2 * i + 1) * step:(2 * i + 2) * step]
+                value = [z[:, columns_of(j)] * scale for j in range(nb)]
+                put(tt, value, r, step, k)
+                if EDGE <= r < end:
+                    for j in range(nw):
+                        tensor_out[k, 0, pl.ds(r - EDGE, step), columns(j)] = value[j]
+
+        if low < EDGE:
+            body(low, EDGE - low)
+        blocks(max(low, EDGE), min(high, end), WIN, body)
+        if high > end:
+            body(end, high - end)
+
+
+    settled = 8 * (SWEEPS - 1)
+
+    def span(c, ahead, margin):
+        low = first + margin if c == 0 else bounds[c] + ahead
+        high = last - margin if c == chunks - 1 else min(bounds[c + 1] + ahead, last - margin)
+        return min(low, high), high
+
+    def beyond_grid(there, at):
         @pl.when(jnp.logical_not(there))
         def _():
             for ref in (gx, gy):
                 clear(ref.at[:, at])
             clear(pr.at[pl.ds(0, 3), :, at])
 
-    def three_rows(ks):
-        def body(r, step):
-            for k in ks:
-                put(p3, add(*(get(pr, r + d, step, k) for d in (-1, 0, 1))), r, step, k)
-
-        return body
-
-    kept = jnp.where(has_next, jnp.float32(1.0), jnp.float32(0.0))
-    cells = float((2 * RADIUS + 1) ** 2)
-
-    src = lax.broadcasted_iota(jnp.int32, (nb * LANES, nb * LANES), 0)
-    dst = lax.broadcasted_iota(jnp.int32, (nb * LANES, nb * LANES), 1)
-    fold_at = nw * LANES + LANES // 2
-    src = jnp.where(src < fold_at, src, src - nb * LANES)
-    dst = jnp.where(dst < fold_at, dst, dst - nb * LANES)
-    band[...] = jnp.where(jnp.abs(src - dst) <= RADIUS, 1.0, 0.0).astype(jnp.bfloat16)
-
-    def window(low, high, ks, factor):
-        scale = kept * (factor / cells)
-
-        def body(r, step):
-            for k in ks:
-                x = jnp.concatenate(add(*(get(p3, r + d, step, k) for d in (-3, 0, 3))), axis=1)
-                coarse = x.astype(jnp.bfloat16)
-                fine = (x - coarse.astype(jnp.float32)).astype(jnp.bfloat16)
-                both = jnp.concatenate([coarse, fine], axis=0)
-                y = jnp.dot(both, band[...], preferred_element_type=jnp.float32)
-                y = (y[:step] + y[step:]) * scale
-                value = [y[:, columns_of(j)] for j in range(nb)]
-                put(tt, value, r, step, k)
-                if EDGE <= r < end:
-                    for j in range(nw):
-                        tensor_out[k, 0, pl.ds(r - EDGE, step), columns(j)] = value[j]
-
-        if low < EDGE:
-            body(low, EDGE - low)
-        blocks(max(low, EDGE), min(high, end), WIN, body)
-        if high > end:
-            body(end, high - end)
-
-    blocks(first, last, 16, three_rows((0, 1, 2)))
-    window(first + 8, last - 8, (0, 1, 2), 0.25)
-
+    def own_products(c):
+        low, high = span(c, settled + 16, 0)
+        blocks(low, high, GRAD, gradient)
+        if c == 0:
+            beyond_grid(has_up, top)
+        if low < last == high:
+            beyond_grid(has_down, bottom)
+        blocks(*span(c, settled + 8, 0), 16, three_rows((0, 1, 2)))
+        window(*span(c, settled, 8), (0, 1, 2), 0.25)
 
     def change(r, step):
         moved = [x - y for x, y in zip(get(b, r, step), get(a, r, step))]
@@ -382,24 +451,23 @@
 
         return body
 
-    def span(c, ahead, margin):
-        low = first + margin if c == 0 else bounds[c] + ahead
-        high = last - margin if c == chunks - 1 else bounds[c + 1] + ahead
-        return low, high
-
     def stages(c, bodies, lead, ends):
         for k, body in enumerate(bodies):
-            blocks(*span(c, 8 * (lead - k), ends[k == len(bodies) - 1]), SWEEP, body)
+            margin = ends[k == len(bodies) - 1]
+            low, high = span(c, 8 * (lead - k), margin)
+            blocks(max(low, first + margin), high, SWEEP, body)
 
     first_round = [setup, sweep(g0, g0, g1), sweep(g1, g0, g2), sweep(g2, g0, g3, field)]
 
     to_next, to_prev = [], []
+    for c in range(min(LEAD, chunks)):
+        own_products(c)
     for c in range(chunks):
         when_got(has_next, tile_b[c])
         if c == 0:
-            when_got(has_next, forward_rows + forward_cols)
-            unpack(b, next_left, next_right, 0)
-        settled = 8 * (SWEEPS - 1)
+            for there, copy in forward_rows + forward_cols:
+                when_got(has_next & there, [copy])
+            unpack(b, next_left, next_right, next_corner, 0)
         blocks(*span(c, settled + 16, 0), 32, change)
         blocks(*span(c, settled + 8, 0), 16, three_rows((3, 4)))
         window(*span(c, settled, 8), (3, 4), 0.5)
@@ -426,6 +494,8 @@
         to_prev.append(moves(rim_after, main_after, prev_id, 2))
         when_start(has_next, to_next[c])
         when_start(has_prev, to_prev[c])
+        if c + LEAD < chunks:
+            own_products(c + LEAD)
 
     def coupled(r, step):
         at = pl.ds(r, step)
@@ -482,7 +552,11 @@
     when_sent(has_down, down)
     when_sent(has_right, [col_right])
     when_sent(has_left, [col_left])
-    when_sent(has_prev, sum(tile_b, []) + forward_rows + forward_cols)
+    for (there, _device), copy in zip(corners, to_corner):
+        when_sent(there, [copy])
+    when_sent(has_prev, sum(tile_b, []))
+    for there, copy in forward_rows + forward_cols:
+        when_sent(has_prev & there, [copy])
 
 
 def pack_rim(field, rim, low, high, first, nw):
@@ -524,7 +598,7 @@
     pair = pltpu.VMEM((2, nb, total, LANES), f32)
     packet = pltpu.VMEM(((rows + 2 * HALO) // FOLD, LANES), f32)
     mains = pltpu.VMEM((2, nw, total, LANES), f32)
-    chunks = (rows + 2 * HALO) // CHUNK
+    chunks = len(bounds_of(rows, 0)) - 1
     results = pl.pallas_call(
         functools.partial(kernel, counts),
         out_shape=(
@@ -537,7 +611,9 @@
         + [five] * 3
         + [plane] * 3
         + [pair] * 7
-        + [packet] * 9
+        + [packet] * 6
+        + [pltpu.VMEM((4, HALO, LANES), f32)] * 2
+        + [packet] * 3
         + [mains] * 2
         + [pltpu.VMEM((nb * LANES, nb * LANES), jnp.bfloat16)]
         + [

time: 25.6 us -> 23.4 us (0.914); the launches traced: 25.5 us -> 23 us
  Pallas kernels: 24.8 us -> 22.4 us
    pallas_call x1, Pallas kernels: 23.5 us -> 21 us  [local(): pl.pallas_call(functools.partial(kernel, counts), out_shape=(jax.ShapeDty...]
where the time goes in v3:
time: 23.4 us; the launch traced here: 23 us
  Pallas kernels  22.4 us (96%)
  between operations  0.64 us (3%)
    pallas_call x1, Pallas kernels, local(): pl.pallas_call(functools.partial(kernel, counts), out_shape=(jax.ShapeDty...  21 us
    pallas_call x1, Pallas kernels, local(): pl.pallas_call(store, out_shape=tuple((jax.ShapeDtypeStruct(x.shape, f32)...  1.31 us

profile of v3, /device:TPU:1, one launch (start us, length us, event | category | flops | bytes accessed | tf_op | source)
XLA Modules:
  0.0 23.0 jit_solution(6750815186688062200)
XLA Ops:
  0.6 21.0 %shard_map.41 = (f32[5,1,256,256]{3,2,1,0:T(8,128)S(1)}, f32[2,1,256,256]{3,2,1,0:T(8,128)S(1)}) custom-call(f32[1,256,256]{2,1,0:T(8,128)} %images.1, f32[1,256,256]{2,1,0:T(8,128)} %stiff.1), custom_call_target="tpu_custom_call" | custom-call | tf_op jit(solution)/shard_map/pallas_call | solution.py:602
  21.7 1.3 %shard_map.42 = (f32[5,1,256,256]{3,2,1,0:T(8,128)}, f32[2,1,256,256]{3,2,1,0:T(8,128)}) custom-call(f32[5,1,256,256]{3,2,1,0:T(8,128)S(1)} %get-tuple-element.4.tensor, f32[2,1,256,256]{3,2,1,0:T(8,128)S(1)} %get-tuple-element.5.field), custom_call_target="tpu_custom_call" | custom-call | tf_op jit(solution)/shard_map/pallas_call | solution.py:632

commit v4 on v3

--- a/solution.py
+++ b/solution.py
@@ -18,8 +18,8 @@
 EDGE = HALO + 8
 LEAD = 9
 GRAD = 16
-WIN = 64
-SWEEP = 32
+WIN = 128
+SWEEP = 16
 EARLY = 2
 SLOT = 16
 CHUNK = 64
@@ -169,6 +169,35 @@
     dst = jnp.where(dst < fold_at, dst, dst - nb * LANES)
     band[...] = jnp.where(jnp.abs(src - dst) <= RADIUS, 1.0, 0.0).astype(jnp.bfloat16)
 
+    def lanes_of(count):
+        return lax.broadcasted_iota(jnp.int32, (count, LANES), 1)
+
+    def packed(to, block, at):
+        for low, high, folds in (
+            (0, HALO, range(1, FOLD)), (HALO, piece - HALO, range(FOLD)),
+            (piece - HALO, piece, range(FOLD - 1)),
+        ):
+            lane = lanes_of(high - low)
+            out = jnp.zeros((high - low, LANES), jnp.float32)
+            for j in folds:
+                span = pl.ds(first + j * piece + low, high - low)
+                for k, ref in enumerate((a, s)):
+                    slot = (2 * j + k) * SLOT
+                    moved = lane_roll(ref[block, span, :], slot - at)
+                    out = jnp.where((lane >= slot) & (lane < slot + SLOT), moved, out)
+            to[pl.ds(low, high - low), :] = out
+
+    for copy in loads:
+        copy.wait()
+
+    @pl.when(has_right)
+    def _():
+        packed(send_right, nw - 1, LANES - SLOT)
+
+    @pl.when(has_left)
+    def _():
+        packed(send_left, 0, 0)
+
     pl.semaphore_wait(barrier, sum(jnp.where(there, 1, 0) for there, _device in sides + corners))
 
     def by_block(src, at, dst, to, k, device):
@@ -196,9 +225,12 @@
         ]
 
     tile_b = [tile_piece(c) for c in range(chunks)]
-    up = by_block(stiff, low, s, bottom, ROW_S_UP, up_id)
+    near = HALO // 2
+    up = by_block(stiff, pl.ds(0, near), s, pl.ds(end, near), ROW_S_UP, up_id)
     up += by_block(images, low, a, bottom, ROW_A_UP, up_id)
-    down = by_block(stiff, high, s, top, ROW_S_DOWN, down_id)
+    down = by_block(
+        stiff, pl.ds(rows - near, near), s, pl.ds(EDGE - near, near), ROW_S_DOWN, down_id
+    )
     down += by_block(images, high, a, top, ROW_A_DOWN, down_id)
     col_right = remote(send_right, got_left, COL_RIGHT, right_id)
     col_left = remote(send_left, got_right, COL_LEFT, left_id)
@@ -242,26 +274,6 @@
     when_start(has_up, up)
     when_start(has_down, down)
     when_start(has_prev, sum(tile_b[:EARLY], []))
-    for copy in loads:
-        copy.wait()
-    def lanes_of(count):
-        return lax.broadcasted_iota(jnp.int32, (count, LANES), 1)
-
-    def packed(to, block, at):
-        for low, high, folds in (
-            (0, HALO, range(1, FOLD)), (HALO, piece - HALO, range(FOLD)),
-            (piece - HALO, piece, range(FOLD - 1)),
-        ):
-            lane = lanes_of(high - low)
-            out = jnp.zeros((high - low, LANES), jnp.float32)
-            for j in folds:
-                span = pl.ds(first + j * piece + low, high - low)
-                for k, ref in enumerate((a, s)):
-                    slot = (2 * j + k) * SLOT
-                    moved = lane_roll(ref[block, span, :], slot - at)
-                    out = jnp.where((lane >= slot) & (lane < slot + SLOT), moved, out)
-            to[pl.ds(low, high - low), :] = out
-
     def rim_of(left, right, j, k):
         lane = lanes_of(right.shape[0])
         slot = (2 * j + k) * SLOT
@@ -281,12 +293,10 @@
 
     @pl.when(has_right)
     def _():
-        packed(send_right, nw - 1, LANES - SLOT)
         col_right.start()
 
     @pl.when(has_left)
     def _():
-        packed(send_left, 0, 0)
         col_left.start()
 
     for (there, _device), copy in zip(corners, to_corner):
@@ -576,11 +586,7 @@
 
 def store(tensor, field, tensor_out, field_out, sem):
     pairs = ((tensor, tensor_out), (field, field_out))
-    copies = [
-        pltpu.make_async_copy(src.at[k], dst.at[k], sem.at[i, k])
-        for i, (src, dst) in enumerate(pairs)
-        for k in range(src.shape[0])
-    ]
+    copies = [pltpu.make_async_copy(src, dst, sem.at[i]) for i, (src, dst) in enumerate(pairs)]
     for copy in copies:
         copy.start()
     for copy in copies:
@@ -634,7 +640,7 @@
         out_shape=tuple(jax.ShapeDtypeStruct(x.shape, f32) for x in results),
         in_specs=[pl.BlockSpec(memory_space=pltpu.VMEM)] * 2,
         out_specs=[pl.BlockSpec(memory_space=pltpu.HBM)] * 2,
-        scratch_shapes=[pltpu.SemaphoreType.DMA((2, 5))],
+        scratch_shapes=[pltpu.SemaphoreType.DMA((2,))],
         compiler_params=pltpu.CompilerParams(vmem_limit_bytes=4 * 1024 * 1024),
     )(*results)
 

time: 23.4 us -> 23.2 us (level)
  no operation moved by 1% of the time
where the time goes in v4:
time: 23.2 us; the launch traced here: 22.8 us
  Pallas kernels  22.2 us (96%)
  between operations  0.64 us (3%)
    pallas_call x1, Pallas kernels, local(): pl.pallas_call(functools.partial(kernel, counts), out_shape=(jax.ShapeDty...  20.9 us
    pallas_call x1, Pallas kernels, local(): pl.pallas_call(store, out_shape=tuple((jax.ShapeDtypeStruct(x.shape, f32)...  1.24 us

profile of v4, /device:TPU:1, one launch (start us, length us, event | category | flops | bytes accessed | tf_op | source)
XLA Modules:
  0.0 22.8 jit_solution(18075872544720244481)
XLA Ops:
  0.6 20.9 %shard_map.41 = (f32[5,1,256,256]{3,2,1,0:T(8,128)S(1)}, f32[2,1,256,256]{3,2,1,0:T(8,128)S(1)}) custom-call(f32[1,256,256]{2,1,0:T(8,128)} %images.1, f32[1,256,256]{2,1,0:T(8,128)} %stiff.1), custom_call_target="tpu_custom_call" | custom-call | tf_op jit(solution)/shard_map/pallas_call | solution.py:608
  21.6 1.2 %shard_map.42 = (f32[5,1,256,256]{3,2,1,0:T(8,128)}, f32[2,1,256,256]{3,2,1,0:T(8,128)}) custom-call(f32[5,1,256,256]{3,2,1,0:T(8,128)S(1)} %get-tuple-element.4.tensor, f32[2,1,256,256]{3,2,1,0:T(8,128)S(1)} %get-tuple-element.5.field), custom_call_target="tpu_custom_call" | custom-call | tf_op jit(solution)/shard_map/pallas_call | solution.py:638

commit v5 on v4

--- a/solution.py
+++ b/solution.py
@@ -20,10 +20,10 @@
 GRAD = 16
 WIN = 128
 SWEEP = 16
-EARLY = 2
+EARLY = 1
 SLOT = 16
 CHUNK = 64
-SHORT = 32
+SHORT = 64
 FOLD = LANES // (2 * SLOT)
 
 (
@@ -301,18 +301,19 @@
 
     for (there, _device), copy in zip(corners, to_corner):
         when_start(there, [copy])
+    when_got(has_left, [col_right])
+    when_got(has_right, [col_left])
+    for there, copy in forward_cols[:2]:
+        when_start(has_prev & there, [copy])
     when_got(has_up, down)
     when_got(has_down, up)
     for there, copy in forward_rows:
         when_start(has_prev & there, [copy])
-    when_start(has_prev, sum(tile_b[EARLY:EARLY + 1], []))
-    when_got(has_left, [col_right])
-    when_got(has_right, [col_left])
     for (there, _device), copy in zip(corners, reversed(to_corner)):
         when_got(there, [copy])
-    for there, copy in forward_cols:
+    for there, copy in forward_cols[2:]:
         when_start(has_prev & there, [copy])
-    when_start(has_prev, sum(tile_b[EARLY + 1:], []))
+    when_start(has_prev, sum(tile_b[EARLY:], []))
     unpack(a, got_left, got_right, corner, 0)
     unpack(s, got_left, got_right, corner, 1)
 

time: 23.2 us -> 22.9 us (0.987)
  no operation moved by 1% of the time
where the time goes in v5:
time: 22.9 us; the launch traced here: 22.7 us
  Pallas kernels  22.1 us (97%)
  between operations  0.64 us (3%)
    pallas_call x1, Pallas kernels, local(): pl.pallas_call(functools.partial(kernel, counts), out_shape=(jax.ShapeDty...  20.8 us
    pallas_call x1, Pallas kernels, local(): pl.pallas_call(store, out_shape=tuple((jax.ShapeDtypeStruct(x.shape, f32)...  1.24 us

profile of v5, /device:TPU:1, one launch (start us, length us, event | category | flops | bytes accessed | tf_op | source)
XLA Modules:
  0.0 22.7 jit_solution(1933236899080788748)
XLA Ops:
  0.6 20.8 %shard_map.41 = (f32[5,1,256,256]{3,2,1,0:T(8,128)S(1)}, f32[2,1,256,256]{3,2,1,0:T(8,128)S(1)}) custom-call(f32[1,256,256]{2,1,0:T(8,128)} %images.1, f32[1,256,256]{2,1,0:T(8,128)} %stiff.1), custom_call_target="tpu_custom_call" | custom-call | tf_op jit(solution)/shard_map/pallas_call | solution.py:609
  21.5 1.2 %shard_map.42 = (f32[5,1,256,256]{3,2,1,0:T(8,128)}, f32[2,1,256,256]{3,2,1,0:T(8,128)}) custom-call(f32[5,1,256,256]{3,2,1,0:T(8,128)S(1)} %get-tuple-element.4.tensor, f32[2,1,256,256]{3,2,1,0:T(8,128)S(1)} %get-tuple-element.5.field), custom_call_target="tpu_custom_call" | custom-call | tf_op jit(solution)/shard_map/pallas_call | solution.py:639

commit v6 on v5

--- a/solution.py
+++ b/solution.py
@@ -271,6 +271,16 @@
             for copy in copies:
                 copy.wait_send()
 
+    for (there, _device), copy in zip(corners, to_corner):
+        when_start(there, [copy])
+    @pl.when(has_right)
+    def _():
+        col_right.start()
+
+    @pl.when(has_left)
+    def _():
+        col_left.start()
+
     when_start(has_up, up)
     when_start(has_down, down)
     when_start(has_prev, sum(tile_b[:EARLY], []))
@@ -291,16 +301,6 @@
         ref[nw, top, :] = rim_of(around[0], around[1], FOLD - 1, k)
         ref[nw, bottom, :] = rim_of(around[2], around[3], 0, k)
 
-    @pl.when(has_right)
-    def _():
-        col_right.start()
-
-    @pl.when(has_left)
-    def _():
-        col_left.start()
-
-    for (there, _device), copy in zip(corners, to_corner):
-        when_start(there, [copy])
     when_got(has_left, [col_right])
     when_got(has_right, [col_left])
     for there, copy in forward_cols[:2]:

time: 22.9 us -> 22.8 us (level)
  no operation moved by 1% of the time
where the time goes in v6:
time: 22.8 us; the launch traced here: 22.7 us
  Pallas kernels  22 us (96%)
  between operations  0.64 us (3%)
    pallas_call x1, Pallas kernels, local(): pl.pallas_call(functools.partial(kernel, counts), out_shape=(jax.ShapeDty...  20.8 us
    pallas_call x1, Pallas kernels, local(): pl.pallas_call(store, out_shape=tuple((jax.ShapeDtypeStruct(x.shape, f32)...  1.24 us

profile of v6, /device:TPU:1, one launch (start us, length us, event | category | flops | bytes accessed | tf_op | source)
XLA Modules:
  0.0 22.7 jit_solution(530237486179718810)
XLA Ops:
  0.6 20.8 %shard_map.41 = (f32[5,1,256,256]{3,2,1,0:T(8,128)S(1)}, f32[2,1,256,256]{3,2,1,0:T(8,128)S(1)}) custom-call(f32[1,256,256]{2,1,0:T(8,128)} %images.1, f32[1,256,256]{2,1,0:T(8,128)} %stiff.1), custom_call_target="tpu_custom_call" | custom-call | tf_op jit(solution)/shard_map/pallas_call | solution.py:609
  21.4 1.2 %shard_map.42 = (f32[5,1,256,256]{3,2,1,0:T(8,128)}, f32[2,1,256,256]{3,2,1,0:T(8,128)}) custom-call(f32[5,1,256,256]{3,2,1,0:T(8,128)S(1)} %get-tuple-element.4.tensor, f32[2,1,256,256]{3,2,1,0:T(8,128)S(1)} %get-tuple-element.5.field), custom_call_target="tpu_custom_call" | custom-call | tf_op jit(solution)/shard_map/pallas_call | solution.py:639

commit v7 on v6

--- a/solution.py
+++ b/solution.py
@@ -20,7 +20,7 @@
 GRAD = 16
 WIN = 128
 SWEEP = 16
-EARLY = 1
+EARLY = 2
 SLOT = 16
 CHUNK = 64
 SHORT = 64

time: 22.8 us -> 22.8 us (level)
  no operation moved by 1% of the time
where the time goes in v7:
time: 22.8 us; the launch traced here: 22.7 us
  Pallas kernels  22 us (96%)
  between operations  0.64 us (3%)
    pallas_call x1, Pallas kernels, local(): pl.pallas_call(functools.partial(kernel, counts), out_shape=(jax.ShapeDty...  20.8 us
    pallas_call x1, Pallas kernels, local(): pl.pallas_call(store, out_shape=tuple((jax.ShapeDtypeStruct(x.shape, f32)...  1.24 us

profile of v7, /device:TPU:1, one launch (start us, length us, event | category | flops | bytes accessed | tf_op | source)
XLA Modules:
  0.0 22.7 jit_solution(15709320613678342031)
XLA Ops:
  0.6 20.8 %shard_map.41 = (f32[5,1,256,256]{3,2,1,0:T(8,128)S(1)}, f32[2,1,256,256]{3,2,1,0:T(8,128)S(1)}) custom-call(f32[1,256,256]{2,1,0:T(8,128)} %images.1, f32[1,256,256]{2,1,0:T(8,128)} %stiff.1), custom_call_target="tpu_custom_call" | custom-call | tf_op jit(solution)/shard_map/pallas_call | solution.py:609
  21.4 1.2 %shard_map.42 = (f32[5,1,256,256]{3,2,1,0:T(8,128)}, f32[2,1,256,256]{3,2,1,0:T(8,128)}) custom-call(f32[5,1,256,256]{3,2,1,0:T(8,128)S(1)} %get-tuple-element.4.tensor, f32[2,1,256,256]{3,2,1,0:T(8,128)S(1)} %get-tuple-element.5.field), custom_call_target="tpu_custom_call" | custom-call | tf_op jit(solution)/shard_map/pallas_call | solution.py:639
